TPU v7x, 256 devices: a whole 4x4x8 slice. The times are simulated.
256 devices in a mesh: seq: 64 (over z, x, core), tp: 4 (over y).
Axes of the slice: x: 4, y: 4, z: 8, core: 2. Of those that a mesh axis runs over, the one named last changes fastest.
Arguments:
- tokens: bfloat16 [32768, 2048], P('seq', 'tp'), may hold values from -6 to 6
- norm_gain: float32 [2048], replicated, may hold values from 0.1 to 1.9
- w_query: bfloat16 [2048, 2048], P(None, 'tp'), may hold values from -0.125 to 0.125
- w_keyval: bfloat16 [2048, 256], replicated, may hold values from -0.125 to 0.125
- w_out: bfloat16 [2048, 2048], P('tp'), may hold values from -0.5 to 0.5
- span_lens: int32 [64], P('seq'), may hold values from 1 to 512, 24576 in all
- cached_lens: int32 [64], P('seq'), may hold values from 1 to 1536, 49152 in all
- old_table: int32 [64, 64], P('seq'), may hold values from 0 to 63, each once within a row
- new_table: int32 [64, 64], P('seq'), may hold values from 0 to 63, each once within a row
- old_cache: bfloat16 [4096, 32, 256], P('seq', 'tp'), may hold values from -720 to 720
Outputs:
- mixed: bfloat16 [32768, 2048], P('seq', 'tp')
- new_cache: bfloat16 [4096, 32, 256], P('seq', 'tp')
Inputs may be any that keep to these rules, and one draw needn't show every extreme that they name: Request r's new tokens are the first span_lens[r] of its 512 rows. `old_table`: each row names every device once: each device holds exactly one block of every request. `new_table`: each row names every device once: each device receives exactly one block of every request.
All inputs are finite; a program needn't handle non-finite values. No bound on the sum of `span_lens` or of `cached_lens` on one device may be relied on, other than what follows from the above.
Results may differ from a plain program's by a relative error of at most 0.012.
The roundings to bfloat16 on the way count: a program that leaves them out, or rounds other values in their place, can miss the bound.
Values may be sent and summed in bfloat16 or wider, within the bound.
A program may use at most 128 MiB of HBM per device.

v0:
```python
import jax
import jax.numpy as jnp
from jax import lax
from jax.sharding import PartitionSpec as P

EPSILON = 1e-05
MASKED = -1e30


def normalize(rows, norm_gain):
    values = rows.astype(jnp.float32)
    average = jnp.mean(values, axis=1, keepdims=True)
    centred = values - average
    spread = jnp.mean(centred * centred, axis=1, keepdims=True)
    return (centred * lax.rsqrt(spread + EPSILON) * norm_gain).astype(jnp.bfloat16)


def body(
    tokens,
    norm_gain,
    w_query,
    w_keyval,
    w_out,
    span_lens,
    cached_lens,
    old_table,
    new_table,
    old_cache,
):
    groups = lax.axis_size("seq")
    tp_count = lax.axis_size("tp")
    tp_index = lax.axis_index("tp")
    holders = old_table[0]
    held_len = cached_lens[0]
    span_len = span_lens[0]
    tok_rows = tokens.shape[0]
    share = old_cache.shape[1]
    width = old_cache.shape[2]
    block_rows = share * tp_count
    capacity = groups * block_rows
    arrived = lax.all_to_all(old_cache, "seq", split_axis=0, concat_axis=0, tiled=True)
    cache_share = jnp.take(arrived, holders, axis=0)
    full_rows = lax.all_gather(tokens, "tp", axis=1, tiled=True)
    normed = normalize(full_rows, norm_gain)
    query = jnp.dot(normed, w_query, preferred_element_type=jnp.float32).astype(jnp.bfloat16)
    keyval = jnp.dot(normed, w_keyval, preferred_element_type=jnp.float32).astype(jnp.bfloat16)
    shifted = lax.dynamic_update_slice(
        jnp.zeros((capacity, width), jnp.bfloat16), keyval, (held_len, jnp.int32(0))
    )
    shifted_share = lax.dynamic_slice_in_dim(
        shifted.reshape(groups, block_rows, width), tp_index * share, share, 1
    )
    share_pos = (
        lax.broadcasted_iota(jnp.int32, (groups, share, 1), 0) * block_rows
        + tp_index * share
        + lax.broadcasted_iota(jnp.int32, (groups, share, 1), 1)
    )
    fresh_share = jnp.where(
        share_pos < held_len,
        cache_share,
        jnp.where(share_pos < held_len + span_len, shifted_share, jnp.zeros_like(shifted_share)),
    )
    targets = new_table[0]
    device_ids = lax.broadcasted_iota(jnp.int32, (groups, groups), 0)
    block_ids = lax.broadcasted_iota(jnp.int32, (groups, groups), 1)
    matches = targets[None, :] == device_ids
    sources = jnp.sum(jnp.where(matches, block_ids, 0), axis=1)
    new_cache = lax.all_to_all(
        jnp.take(fresh_share, sources, axis=0), "seq", split_axis=0, concat_axis=0, tiled=True
    )
    cached = lax.all_gather(cache_share, "tp", axis=1, tiled=True).reshape(capacity, width)
    positions = lax.broadcasted_iota(jnp.int32, (capacity, 1), 0)
    fresh = jnp.where(
        positions < held_len,
        cached,
        jnp.where(positions < held_len + span_len, shifted, jnp.zeros_like(shifted)),
    )
    head_size = width // 2
    keys = fresh[:, :head_size]
    values = fresh[:, head_size:]
    local_heads = query.shape[1] // head_size
    query3 = query.reshape(tok_rows, local_heads, head_size)
    scores = jnp.einsum(
        "thd,kd->htk", query3, keys, preferred_element_type=jnp.float32
    ) * head_size ** (-0.5)
    row_pos = lax.broadcasted_iota(jnp.int32, (tok_rows, 1), 0)
    key_pos = lax.broadcasted_iota(jnp.int32, (1, capacity), 1)
    allowed = key_pos <= held_len + row_pos
    scores = jnp.where(allowed[None], scores, MASKED)
    top = jnp.max(scores, axis=2, keepdims=True)
    weights = jnp.exp(scores - top)
    probs = (weights / jnp.sum(weights, axis=2, keepdims=True)).astype(jnp.bfloat16)
    context = jnp.einsum("htk,kd->thd", probs, values, preferred_element_type=jnp.float32).astype(
        jnp.bfloat16
    )
    context = context.reshape(tok_rows, local_heads * head_size)
    partial_out = jnp.dot(context, w_out, preferred_element_type=jnp.float32)
    summed = lax.psum_scatter(
        partial_out.astype(jnp.bfloat16), "tp", scatter_dimension=1, tiled=True
    ).astype(jnp.float32)
    total = tokens.astype(jnp.float32) + summed
    mixed = jnp.where(row_pos < span_len, total, jnp.zeros_like(total)).astype(jnp.bfloat16)
    return (mixed, new_cache)


def solution(mesh):
    in_specs = (
        P("seq", "tp"),
        P(),
        P(None, "tp"),
        P(),
        P("tp", None),
        P("seq"),
        P("seq"),
        P("seq", None),
        P("seq", None),
        P("seq", "tp", None),
    )
    out_specs = (P("seq", "tp"), P("seq", "tp", None))
    return jax.shard_map(body, mesh=mesh, in_specs=in_specs, out_specs=out_specs, check_vma=False)
```

profile of v0, /device:TPU:1, one launch (start us, length us, event | category | flops | bytes accessed | tf_op | source)
XLA Modules:
  0.0 153.1 jit_solution(9230389170875504754)
XLA Ops:
  7.2 0.0 copy-start
  7.2 0.0 copy-start.5
  7.2 0.0 all-gather.5.cloned.1.call-start
  7.2 0.7 all-gather.5.cloned.1.call-update
  7.9 13.0 %all-to-all-start = ((bf16[64,8,256]{2,1,0:T(8,128)(2,1)}), bf16[64,8,256]{2,1,0:T(8,128)(2,1)S(1)}, u32[]{:S(2)}, u32[]{:S(2)}) async-start(bf16[64,8,256]{2,1,0:T(8,128)(2,1)} %param.21), calls=%async_computation | async-start | bytes 524288 | tf_op jit(solution)/shard_map/all_to_all | solution.py:41
  20.9 0.0 all-gather.3.cloned.1.call-start
  22.3 0.7 compare_select_fusion.1
  23.0 0.7 compare_and_fusion.1
  23.6 0.1 fusion.16
  23.7 10.4 %all-to-all-done = bf16[64,8,256]{2,1,0:T(8,128)(2,1)S(1)} async-done(((bf16[64,8,256]{2,1,0:T(8,128)(2,1)}), bf16[64,8,256]{2,1,0:T(8,128)(2,1)S(1)}, u32[]{:S(2)}, u32[]{:S(2)}) %all-to-all-start) | async-done | bytes 262176 | tf_op jit(solution)/shard_map/all_to_all | solution.py:41
  34.1 1.3 gather_fusion
  35.4 11.7 %all-gather.5.cloned.1.call-done = bf16[512,2048]{1,0:T(8,128)(2,1)} async-done(((bf16[512,512]{1,0:T(8,128)(2,1)}), bf16[512,2048]{1,0:T(8,128)(2,1)}) %all-gather.5.cloned.1.call-update) | async-done | bytes 2097168 | tf_op jit(solution)/shard_map/all_gather | solution.py:43
  47.1 2.1 %convert_reduce_fusion = f32[512]{0:T(512)S(1)} fusion(bf16[512,2048]{1,0:T(8,128)(2,1)} %all-gather.5.cloned.1.call-done), kind=kLoop, calls=%fused_computation.12 | loop fusion | flops 2096640 | bytes 2099200 | tf_op jit(solution)/shard_map/reduce_sum | solution.py:12
  49.2 2.3 %fusion.8 = f32[512]{0:T(512)S(1)} fusion(bf16[512,2048]{1,0:T(8,128)(2,1)} %all-gather.5.cloned.1.call-done, f32[512]{0:T(512)S(1)} %broadcast_multiply_fusion), kind=kLoop, calls=%fused_computation.15 | loop fusion | flops 4193792 | bytes 2101248 | tf_op jit(solution)/shard_map/reduce_sum | solution.py:14
  51.5 0.0 copy-done.5
  51.5 0.0 copy-done.1
  51.5 0.7 fusion.10
  52.2 0.0 copy-done.6
  52.3 0.0 copy-start.2
  52.3 0.7 convolution_convert_fusion.2
  53.0 0.6 copy-done.2
  53.6 0.1 broadcast.104
  53.7 1.9 %dynamic_update_slice.3 = bf16[2048,256]{1,0:T(8,128)(2,1)S(1)} dynamic-update-slice(bf16[2048,256]{1,0:T(8,128)(2,1)S(1)} %broadcast.104, bf16[512,256]{1,0:T(8,128)(2,1)S(1)} %convolution_convert_fusion.2, s32[]{:T(128)S(6)} %select_n.39, s32[]{:T(128)} %constant.9.clone.1) | dynamic-update-slice | bytes 524292 | tf_op jit(solution)/shard_map/dynamic_update_slice | solution.py:47
  55.6 1.9 %select_select_fusion = (bf16[64,8,256]{2,1,0:T(8,128)(2,1)S(1)}, bf16[64,8,256]{2,1,0:T(8,128)(2,1)}) fusion(bf16[64,32,256]{2,1,0:T(8,128)(2,1)S(1)} %bitcast.57, s32[]{:T(128)S(6)} %select_n.44, pred[64,8]{1,0:T(8,128)(4,1)S(1)} %get-tuple-element.6, pred[64,8]{1,0:T(8,128)(4,1)S(1)} %get-tuple-element.5, bf16[64,8,256]{2,1,0:T(8,128)(2,1)} %gather_fusion, ...), kind=kLoop, calls=%fused_computation.29 | loop fusion | flops 393216 | bytes 1049668 | tf_op jit(solution)/shard_map/jit(_where)/select_n | solution.py:58
  57.5 0.0 all-gather.3.cloned.1.call-update
  57.5 0.2 reduce-scatter.2.cloned.1.call-start
  57.8 1.8 %iota_compare_fusion = pred[512,2048]{0,1:T(8,128)(4,1)} fusion(s32[512]{0:T(512)S(1)} %iota_add_fusion.1), kind=kLoop, calls=%fused_computation.18 | loop fusion | flops 1048576 | bytes 1050624 | tf_op jit(solution)/shard_map/le | solution.py:88
  59.6 4.3 %convolution_convert_fusion.1 = bf16[512,512]{0,1:T(8,128)(2,1)} fusion(bf16[512,2048]{1,0:T(8,128)(2,1)} %copy-done.2, bf16[2048,512]{1,0:T(8,128)(2,1)} %param.14), kind=kOutput, calls=%fused_computation.21 | convolution fusion | flops 1074003968 | bytes 4718592 | tf_op jit(solution)/shard_map/dot_general | solution.py:45
  63.9 21.4 %all-gather.3.cloned.1.call-done = bf16[64,32,256]{2,1,0:T(8,128)(2,1)} async-done(((bf16[64,8,256]{2,1,0:T(8,128)(2,1)}), bf16[64,32,256]{2,1,0:T(8,128)(2,1)}) %all-gather.3.cloned.1.call-update) | async-done | bytes 1048592 | tf_op jit(solution)/shard_map/all_gather | solution.py:71
  85.3 3.8 %bitcast_select_fusion.4 = bf16[2048,256]{1,0:T(8,128)(2,1)} fusion(bf16[64,32,256]{2,1,0:T(8,128)(2,1)} %all-gather.3.cloned.1.call-done, bf16[2048,256]{1,0:T(8,128)(2,1)S(1)} %dynamic_update_slice.3, pred[2048]{0:T(1024)(128)(4,1)S(1)} %get-tuple-element.9, pred[2048]{0:T(1024)(128)(4,1)S(1)} %get-tuple-element.10), kind=kLoop, calls=%fused_computation.24 | loop fusion | flops 1048576 | bytes 3149824 | tf_op jit(solution)/shard_map/jit(_where)/select_n | solution.py:73
  89.1 10.7 %fusion.19 = (f32[4,512]{1,0:T(4,128)S(1)}, f32[4,512,2048]{1,2,0:T(8,128)}) fusion(pred[512,2048]{0,1:T(8,128)(4,1)} %iota_compare_fusion, bf16[512,4,128]{0,2,1:T(8,128)(2,1)} %bitcast.59, bf16[2048,256]{1,0:T(8,128)(2,1)} %bitcast_select_fusion.4), kind=kOutput, calls=%fused_computation.52 | convolution fusion | flops 1090521088 | bytes 18882560 | tf_op jit(solution)/shard_map/sub | solution.py:91
  99.8 0.0 copy-done.4
  99.8 7.0 %fusion.13 = bf16[128,4,512]{2,0,1:T(8,128)(2,1)S(1)} fusion(f32[4,512,2048]{1,2,0:T(8,128)} %get-tuple-element.8, f32[4,512]{1,0:T(4,128)S(1)} %get-tuple-element.7, bf16[2048,256]{1,0:T(8,128)(2,1)S(1)} %copy-done.4), kind=kOutput, calls=%fused_computation.22 | convolution fusion | flops 1082392576 | bytes 17833984 | tf_op jit(solution)/shard_map/htk,kd->thd/dot_general | solution.py:93
  106.8 0.0 copy-start.7
  106.8 0.0 copy-done
  106.9 0.0 copy-start.3
  106.9 2.6 %convolution_convert_fusion = bf16[512,2048]{1,0:T(8,128)(2,1)} fusion(bf16[512,512]{0,1:T(8,128)(2,1)S(1)} %bitcast.60, bf16[512,2048]{1,0:T(8,128)(2,1)S(1)} %copy-done), kind=kOutput, calls=%fused_computation.19 | convolution fusion | flops 1074790400 | bytes 4718592 | tf_op jit(solution)/shard_map/dot_general | solution.py:97
  109.5 0.0 reduce-scatter.2.cloned.1.call-update
  109.5 0.0 copy-done.7
  109.5 0.1 select_reduce_fusion
  109.7 0.6 gather_fusion.1
  110.3 0.8 broadcast_select_fusion
  111.1 11.5 %all-to-all-start.1 = ((bf16[64,8,256]{2,1,0:T(8,128)(2,1)}), bf16[64,8,256]{2,1,0:T(8,128)(2,1)S(1)}, u32[]{:S(2)}, u32[]{:S(2)}) async-start(bf16[64,8,256]{2,1,0:T(8,128)(2,1)} %broadcast_select_fusion), calls=%async_computation.2 | async-start | bytes 524288 | tf_op jit(solution)/shard_map/all_to_all | solution.py:68
  122.7 13.1 %all-to-all-done.1 = bf16[64,8,256]{2,1,0:T(8,128)(2,1)S(1)} async-done(((bf16[64,8,256]{2,1,0:T(8,128)(2,1)}), bf16[64,8,256]{2,1,0:T(8,128)(2,1)S(1)}, u32[]{:S(2)}, u32[]{:S(2)}) %all-to-all-start.1) | async-done | bytes 262176 | tf_op jit(solution)/shard_map/all_to_all | solution.py:68
  135.8 8.0 %reduce-scatter.2.cloned.1.call-done = bf16[512,512]{1,0:T(8,128)(2,1)} async-done(((bf16[512,2048]{1,0:T(8,128)(2,1)}), bf16[512,512]{1,0:T(8,128)(2,1)}) %reduce-scatter.2.cloned.1.call-update) | async-done | bytes 524304 | tf_op jit(solution)/shard_map/reduce_scatter | solution.py:98
  143.8 0.0 copy-done.3
  143.8 2.0 %select_convert_fusion = bf16[512,512]{1,0:T(8,128)(2,1)} fusion(bf16[512,512]{1,0:T(8,128)(2,1)} %reduce-scatter.2.cloned.1.call-done, bf16[512,512]{1,0:T(8,128)(2,1)S(1)} %copy-done.3, pred[512]{0:T(512)(128)(4,1)S(1)} %iota_compare_fusion.4), kind=kLoop, calls=%fused_computation.25 | loop fusion | flops 1310720 | bytes 1573376 | tf_op jit(solution)/shard_map/convert_element_type | solution.py:102
  145.9 0.7 copy.29
  (13 shorter events, 0.1 us)
Async XLA Ops:
  7.2 99.7 %copy-start = (bf16[512,2048]{1,0:T(8,128)(2,1)S(1)}, bf16[512,2048]{1,0:T(8,128)(2,1)}, u32[]{:S(2)}) copy-start(bf16[512,2048]{1,0:T(8,128)(2,1)} %param.16) | copy-start | bytes 6291460
  7.2 44.3 %copy-start.5 = (f32[2048]{0:T(1024)S(1)}, f32[2048]{0:T(1024)}, u32[]{:S(2)}) copy-start(f32[2048]{0:T(1024)} %param.13) | copy-start | bytes 24580
  7.2 39.9 %all-gather.5.cloned.1.call-start = ((), (), s32[]{:S(2)}) async-start(), calls=%async_computation.4 | async-start | bytes 2621440 | tf_op jit(solution)/shard_map/all_gather | solution.py:43
  7.9 26.2 %all-to-all-start = ((bf16[64,8,256]{2,1,0:T(8,128)(2,1)}), bf16[64,8,256]{2,1,0:T(8,128)(2,1)S(1)}, u32[]{:S(2)}, u32[]{:S(2)}) async-start(bf16[64,8,256]{2,1,0:T(8,128)(2,1)} %param.21), calls=%async_computation | async-start | bytes 524288 | tf_op jit(solution)/shard_map/all_to_all | solution.py:41
  20.9 64.3 %all-gather.3.cloned.1.call-start = ((), (), s32[]{:S(2)}) async-start(), calls=%async_computation.3 | async-start | bytes 1310720 | tf_op jit(solution)/shard_map/all_gather | solution.py:71
  47.1 4.4 %copy-start.1 = (bf16[512,2048]{1,0:T(8,128)(2,1)S(1)}, bf16[512,2048]{1,0:T(8,128)(2,1)}, u32[]{:S(2)}) copy-start(bf16[512,2048]{1,0:T(8,128)(2,1)} %all-gather.5.cloned.1.call-done) | copy-start | bytes 6291460
  47.1 5.1 %copy-start.6 = (bf16[2048,256]{1,0:T(8,128)(2,1)S(1)}, bf16[2048,256]{1,0:T(8,128)(2,1)}, u32[]{:S(2)}) copy-start(bf16[2048,256]{1,0:T(8,128)(2,1)} %param.15) | copy-start | bytes 3145732
  52.3 1.3 copy-start.2
  57.5 86.3 %reduce-scatter.2.cloned.1.call-start = ((), (), s32[]{:S(2)}) async-start(), calls=%async_computation.5 | async-start | bytes 2621440 | tf_op jit(solution)/shard_map/reduce_scatter | solution.py:98
  89.1 10.7 %copy-start.4 = (bf16[2048,256]{1,0:T(8,128)(2,1)S(1)}, bf16[2048,256]{1,0:T(8,128)(2,1)}, u32[]{:S(2)}) copy-start(bf16[2048,256]{1,0:T(8,128)(2,1)} %bitcast_select_fusion.4) | copy-start | bytes 3145732
  106.8 2.7 %copy-start.7 = (s32[1,64]{1,0:T(1,128)S(1)}, s32[1,64]{1,0:T(1,128)}, u32[]{:S(2)}) copy-start(s32[1,64]{1,0:T(1,128)} %param.20) | copy-start | bytes 772
  106.9 37.0 %copy-start.3 = (bf16[512,512]{1,0:T(8,128)(2,1)S(1)}, bf16[512,512]{1,0:T(8,128)(2,1)}, u32[]{:S(2)}) copy-start(bf16[512,512]{1,0:T(8,128)(2,1)} %param.12) | copy-start | bytes 1572868
  111.1 24.7 %all-to-all-start.1 = ((bf16[64,8,256]{2,1,0:T(8,128)(2,1)}), bf16[64,8,256]{2,1,0:T(8,128)(2,1)S(1)}, u32[]{:S(2)}, u32[]{:S(2)}) async-start(bf16[64,8,256]{2,1,0:T(8,128)(2,1)} %broadcast_select_fusion), calls=%async_computation.2 | async-start | bytes 524288 | tf_op jit(solution)/shard_map/all_to_all | solution.py:68
Sparse Core Ops, SparseCore 0:
  9.8 37.2 all-gather.4
  57.6 27.5 all-gather.2
  109.6 34.1 reduce-scatter.1
where the time goes:
time: 154 us; the launch traced here: 153 us
  waiting for transfers between devices  65.4 us (42%)
  matrix products  25.4 us (16%)
  starting transfers between devices  24.8 us (16%)
  other arithmetic  17 us (11%)
  between operations  15.3 us (10%)
  local copies, waits for them, and re-layouts  5.21 us (3%)
    all_gather x1, waiting for transfers between devices, body(): lax.all_gather(cache_share, 'tp', axis=1, tiled=True)  21.4 us
    all_to_all x1, waiting for transfers between devices, body(): lax.all_to_all(jnp.take(fresh_share, sources, axis=0), 'seq', split_axis=...  13.1 us
    all_to_all x1, starting transfers between devices, body(): lax.all_to_all(old_cache, 'seq', split_axis=0, concat_axis=0, tiled=True)  13 us
    all_gather x1, waiting for transfers between devices, body(): full_rows = lax.all_gather(tokens, 'tp', axis=1, tiled=True)  11.7 us
    all_to_all x1, starting transfers between devices, body(): lax.all_to_all(jnp.take(fresh_share, sources, axis=0), 'seq', split_axis=...  11.5 us
    sub x1, matrix products, body(): weights = jnp.exp(scores - top)  10.7 us
    all_to_all x1, waiting for transfers between devices, body(): lax.all_to_all(old_cache, 'seq', split_axis=0, concat_axis=0, tiled=True)  10.4 us
    reduce_scatter x1, waiting for transfers between devices, body(): lax.psum_scatter(partial_out.astype(jnp.bfloat16), 'tp', scatter_dimensio...  8.03 us
  transfers between devices with their start and end apart: 5, of which 5 were waited for; matrix products, arithmetic and copies ran while one was open for 7% of the time, Pallas kernels for 0%

commit v1 on v0

--- a/solution.py
+++ b/solution.py
@@ -40,7 +40,16 @@
     capacity = groups * block_rows
     arrived = lax.all_to_all(old_cache, "seq", split_axis=0, concat_axis=0, tiled=True)
     cache_share = jnp.take(arrived, holders, axis=0)
-    full_rows = lax.all_gather(tokens, "tp", axis=1, tiled=True)
+    ways = lax.axis_size("tp")
+    up = [(d, (d + 1) % ways) for d in range(ways)]
+    down = [(d, (d - 1) % ways) for d in range(ways)]
+    earlier, later = ([tokens], [tokens])
+    for _ in range(ways // 2):
+        earlier.append(lax.ppermute(earlier[-1], "tp", up))
+    for _ in range((ways - 1) // 2):
+        later.append(lax.ppermute(later[-1], "tp", down))
+    line = jnp.concatenate([*earlier[::-1], *later[1:]], axis=1)
+    full_rows = jnp.roll(line, (lax.axis_index("tp") - ways // 2) * tokens.shape[1], axis=1)
     normed = normalize(full_rows, norm_gain)
     query = jnp.dot(normed, w_query, preferred_element_type=jnp.float32).astype(jnp.bfloat16)
     keyval = jnp.dot(normed, w_keyval, preferred_element_type=jnp.float32).astype(jnp.bfloat16)

time: 154 us -> 148 us (0.961)
  waiting for transfers between devices: 65.4 us -> 54 us
  local copies, waits for them, and re-layouts: 5.21 us -> 10.3 us
  starting transfers between devices: 24.8 us -> 28.3 us
  other arithmetic: 17 us -> 13.6 us
    all_gather x1 -> x0, waiting for transfers between devices: 11.7 us -> none  [body(): full_rows = lax.all_gather(tokens, 'tp', axis=1, tiled=True)]
    unnamed x17 -> x22, local copies, waits for them, and re-layouts: 1.35 us -> 6.43 us
    ppermute x0 -> x3, starting transfers between devices: none -> 3.9 us  [the longest x2 2.37 us: body(): earlier.append(lax.ppermute(earlier[-1], 'tp', up))]
    ppermute x0 -> x3, waiting for transfers between devices: none -> 2.43 us  [the longest x2 2.43 us: body(): earlier.append(lax.ppermute(earlier[-1], 'tp', up))]
    reduce_sum x1, other arithmetic: 2.09 us -> 0.36 us  [normalize(): average = jnp.mean(values, axis=1, keepdims=True)]
    reduce_sum x1, other arithmetic: 2.27 us -> 0.69 us  [normalize(): spread = jnp.mean(centred * centred, axis=1, keepdims=True)]
  transfers between devices with their start and end apart: 5 -> 7, of which waited for: 5 -> 5; matrix products, arithmetic and copies ran while one was open for 7% -> 10% of each run, Pallas kernels for 0% -> 0%
where the time goes in v1:
time: 148 us
  waiting for transfers between devices  54 us (36%)
  starting transfers between devices  28.3 us (19%)
  matrix products  25.7 us (17%)
  between operations  15.6 us (11%)
  other arithmetic  13.6 us (9%)
  local copies, waits for them, and re-layouts  10.3 us (7%)
    all_gather x1, waiting for transfers between devices, body(): lax.all_gather(cache_share, 'tp', axis=1, tiled=True)  20.8 us
    all_to_all x1, waiting for transfers between devices, body(): lax.all_to_all(jnp.take(fresh_share, sources, axis=0), 'seq', split_axis=...  13.2 us
    all_to_all x1, starting transfers between devices, body(): lax.all_to_all(old_cache, 'seq', split_axis=0, concat_axis=0, tiled=True)  12.6 us
    all_to_all x1, starting transfers between devices, body(): lax.all_to_all(jnp.take(fresh_share, sources, axis=0), 'seq', split_axis=...  11.5 us
    sub x1, matrix products, body(): weights = jnp.exp(scores - top)  10.7 us
    all_to_all x1, waiting for transfers between devices, body(): lax.all_to_all(old_cache, 'seq', split_axis=0, concat_axis=0, tiled=True)  9.44 us
    reduce_scatter x1, waiting for transfers between devices, body(): lax.psum_scatter(partial_out.astype(jnp.bfloat16), 'tp', scatter_dimensio...  8.13 us
    dot_general x1, matrix products, body(): jnp.einsum('htk,kd->thd', probs, values, preferred_element_type=jnp.float32)  7.05 us
  transfers between devices with their start and end apart: 7, of which 5 were waited for; matrix products, arithmetic and copies ran while one was open for 10% of the time, Pallas kernels for 0%

profile of v1, /device:TPU:1, one launch (start us, length us, event | category | flops | bytes accessed | tf_op | source)
XLA Modules:
  0.0 147.6 jit_solution(7710496070071526802)
XLA Ops:
  7.2 0.0 copy-start
  7.2 0.0 copy-start.2
  7.2 2.2 %collective-permute-start = (bf16[512,512]{1,0:T(8,128)(2,1)}, bf16[512,512]{1,0:T(8,128)(2,1)}, u32[]{:S(2)}, u32[]{:S(2)}) collective-permute-start(bf16[512,512]{1,0:T(8,128)(2,1)} %param.12), channel_id=1, source_target_pairs={{0,1},{1,2},{2,3},{3,0},{4,5},{5,6},{6,7},{7,4},{8,9},{9,10},{10,1... | collective-permute-start | bytes 1572872 | tf_op jit(solution)/shard_map/ppermute | solution.py:48
  9.4 1.5 %collective-permute-start.2 = (bf16[512,512]{1,0:T(8,128)(2,1)}, bf16[512,512]{1,0:T(8,128)(2,1)S(1)}, u32[]{:S(2)}, u32[]{:S(2)}) collective-permute-start(bf16[512,512]{1,0:T(8,128)(2,1)} %param.12), channel_id=1, source_target_pairs={{0,3},{1,0},{2,1},{3,2},{4,7},{5,4},{6,5},{7,6},{8,11},{9,8},{10,9... | collective-permute-start | bytes 1572872 | tf_op jit(solution)/shard_map/ppermute | solution.py:50
  10.9 12.6 %all-to-all-start = ((bf16[64,8,256]{2,1,0:T(8,128)(2,1)}), bf16[64,8,256]{2,1,0:T(8,128)(2,1)S(1)}, u32[]{:S(2)}, u32[]{:S(2)}) async-start(bf16[64,8,256]{2,1,0:T(8,128)(2,1)} %param.21), calls=%async_computation | async-start | bytes 524288 | tf_op jit(solution)/shard_map/all_to_all | solution.py:41
  23.5 0.0 all-gather.2.cloned.1.call-start
  24.9 0.8 select_reduce_fusion
  25.6 0.1 fusion.16
  25.7 0.2 collective-permute-start.1
  25.9 0.7 compare_select_fusion
  26.6 0.7 compare_and_fusion.1
  27.2 9.4 %all-to-all-done = bf16[64,8,256]{2,1,0:T(8,128)(2,1)S(1)} async-done(((bf16[64,8,256]{2,1,0:T(8,128)(2,1)}), bf16[64,8,256]{2,1,0:T(8,128)(2,1)S(1)}, u32[]{:S(2)}, u32[]{:S(2)}) %all-to-all-start) | async-done | bytes 262176 | tf_op jit(solution)/shard_map/all_to_all | solution.py:41
  36.7 1.3 gather_fusion
  38.0 2.4 %collective-permute-done.1 = bf16[512,512]{1,0:T(8,128)(2,1)} collective-permute-done((bf16[512,512]{1,0:T(8,128)(2,1)}, bf16[512,512]{1,0:T(8,128)(2,1)}, u32[]{:S(2)}, u32[]{:S(2)}) %collective-permute-start.1) | collective-permute-done | bytes 524320 | tf_op jit(solution)/shard_map/ppermute | solution.py:48
  40.4 1.1 constant_dynamic-update-slice_fusion.7
  41.5 1.1 constant_dynamic-update-slice_fusion.6
  42.6 1.1 constant_dynamic-update-slice_fusion.5
  43.7 0.1 constant_dynamic-update-slice_fusion.4
  43.8 0.0 copy-start.6
  43.8 1.2 constant_dynamic-update-slice_fusion.3
  45.0 1.1 constant_dynamic-update-slice_fusion.2
  46.1 0.1 constant_dynamic-update-slice_fusion.1
  46.2 0.1 constant_dynamic-update-slice_fusion
  46.2 0.4 convert_reduce_fusion
  46.6 0.7 fusion.8
  47.3 0.8 convolution_convert_fusion.2
  48.2 0.0 copy-done.1
  48.2 0.1 broadcast.105
  48.2 1.9 %dynamic_update_slice.3 = bf16[2048,256]{1,0:T(8,128)(2,1)S(1)} dynamic-update-slice(bf16[2048,256]{1,0:T(8,128)(2,1)S(1)} %broadcast.105, bf16[512,256]{1,0:T(8,128)(2,1)S(1)} %convolution_convert_fusion.2, s32[]{:T(128)S(6)} %select_n.54, s32[]{:T(128)} %constant.22.clone.1) | dynamic-update-slice | bytes 524292 | tf_op jit(solution)/shard_map/dynamic_update_slice | solution.py:56
  50.1 1.9 %select_select_fusion = (bf16[64,8,256]{2,1,0:T(8,128)(2,1)S(1)}, bf16[64,8,256]{2,1,0:T(8,128)(2,1)}) fusion(bf16[64,32,256]{2,1,0:T(8,128)(2,1)S(1)} %bitcast.55, s32[]{:T(128)S(6)} %select_n.59, pred[64,8]{1,0:T(8,128)(4,1)S(1)} %get-tuple-element.6, pred[64,8]{1,0:T(8,128)(4,1)S(1)} %get-tuple-element.5, bf16[64,8,256]{2,1,0:T(8,128)(2,1)} %gather_fusion, ...), kind=kLoop, calls=%fused_computation.29 | loop fusion | flops 393216 | bytes 1049668 | tf_op jit(solution)/shard_map/jit(_where)/select_n | solution.py:67
  52.1 0.0 all-gather.2.cloned.1.call-update
  52.1 0.2 reduce-scatter.2.cloned.1.call-start
  52.3 1.8 %iota_compare_fusion = pred[512,2048]{0,1:T(8,128)(4,1)} fusion(s32[512]{0:T(512)S(1)} %iota_add_fusion.1), kind=kLoop, calls=%fused_computation.18 | loop fusion | flops 1048576 | bytes 1050624 | tf_op jit(solution)/shard_map/le | solution.py:97
  54.1 4.5 %convolution_convert_fusion.1 = bf16[512,512]{0,1:T(8,128)(2,1)} fusion(bf16[2048,512]{1,0:T(8,128)(2,1)} %param.14, f32[2048]{0:T(1024)S(1)} %copy-done.6, f32[512]{0:T(512)S(1)} %add_rsqrt_fusion, f32[512]{0:T(512)S(1)} %broadcast_multiply_fusion, bf16[512,4096]{1,0:T(8,128)(2,1)} %copy-done.1, s32[]{:T(128)S(6)} %select_n.53), kind=kOutput, calls=%fused_computation.21 | convolution fusion | flops 1079246848 | bytes 4730884 | tf_op jit(solution)/shard_map/dot_general | solution.py:54
  58.6 20.8 %all-gather.2.cloned.1.call-done = bf16[64,32,256]{2,1,0:T(8,128)(2,1)} async-done(((bf16[64,8,256]{2,1,0:T(8,128)(2,1)}), bf16[64,32,256]{2,1,0:T(8,128)(2,1)}) %all-gather.2.cloned.1.call-update) | async-done | bytes 1048592 | tf_op jit(solution)/shard_map/all_gather | solution.py:80
  79.4 3.8 %bitcast_select_fusion.4 = bf16[2048,256]{1,0:T(8,128)(2,1)} fusion(bf16[64,32,256]{2,1,0:T(8,128)(2,1)} %all-gather.2.cloned.1.call-done, bf16[2048,256]{1,0:T(8,128)(2,1)S(1)} %dynamic_update_slice.3, pred[2048]{0:T(1024)(128)(4,1)S(1)} %get-tuple-element.11, pred[2048]{0:T(1024)(128)(4,1)S(1)} %get-tuple-element.12), kind=kLoop, calls=%fused_computation.24 | loop fusion | flops 1048576 | bytes 3149824 | tf_op jit(solution)/shard_map/jit(_where)/select_n | solution.py:82
  83.2 10.7 %fusion.21 = (f32[4,512]{1,0:T(4,128)S(1)}, f32[4,512,2048]{1,2,0:T(8,128)}) fusion(pred[512,2048]{0,1:T(8,128)(4,1)} %iota_compare_fusion, bf16[512,4,128]{0,2,1:T(8,128)(2,1)} %bitcast.57, bf16[2048,256]{1,0:T(8,128)(2,1)} %bitcast_select_fusion.4), kind=kOutput, calls=%fused_computation.60 | convolution fusion | flops 1090521088 | bytes 18882560 | tf_op jit(solution)/shard_map/sub | solution.py:100
  93.9 7.0 %fusion.13 = bf16[128,4,512]{2,0,1:T(8,128)(2,1)S(1)} fusion(f32[4,512,2048]{1,2,0:T(8,128)} %get-tuple-element.8, f32[4,512]{1,0:T(4,128)S(1)} %get-tuple-element.7, bf16[2048,256]{1,0:T(8,128)(2,1)S(1)} %copy-done.4), kind=kOutput, calls=%fused_computation.22 | convolution fusion | flops 1082392576 | bytes 17833984 | tf_op jit(solution)/shard_map/htk,kd->thd/dot_general | solution.py:102
  101.0 0.0 copy-start.3
  101.0 2.6 %convolution_convert_fusion = bf16[512,2048]{1,0:T(8,128)(2,1)} fusion(bf16[512,512]{0,1:T(8,128)(2,1)S(1)} %bitcast.58, bf16[512,2048]{1,0:T(8,128)(2,1)S(1)} %copy-done), kind=kOutput, calls=%fused_computation.19 | convolution fusion | flops 1074790400 | bytes 4718592 | tf_op jit(solution)/shard_map/dot_general | solution.py:106
  103.7 0.0 reduce-scatter.2.cloned.1.call-update
  103.7 0.6 gather_fusion.1
  104.3 0.8 broadcast_select_fusion
  105.2 11.5 %all-to-all-start.1 = ((bf16[64,8,256]{2,1,0:T(8,128)(2,1)}), bf16[64,8,256]{2,1,0:T(8,128)(2,1)S(1)}, u32[]{:S(2)}, u32[]{:S(2)}) async-start(bf16[64,8,256]{2,1,0:T(8,128)(2,1)} %broadcast_select_fusion), calls=%async_computation.2 | async-start | bytes 524288 | tf_op jit(solution)/shard_map/all_to_all | solution.py:77
  116.7 13.2 %all-to-all-done.1 = bf16[64,8,256]{2,1,0:T(8,128)(2,1)S(1)} async-done(((bf16[64,8,256]{2,1,0:T(8,128)(2,1)}), bf16[64,8,256]{2,1,0:T(8,128)(2,1)S(1)}, u32[]{:S(2)}, u32[]{:S(2)}) %all-to-all-start.1) | async-done | bytes 262176 | tf_op jit(solution)/shard_map/all_to_all | solution.py:77
  129.9 8.1 %reduce-scatter.2.cloned.1.call-done = bf16[512,512]{1,0:T(8,128)(2,1)} async-done(((bf16[512,2048]{1,0:T(8,128)(2,1)}), bf16[512,512]{1,0:T(8,128)(2,1)}) %reduce-scatter.2.cloned.1.call-update) | async-done | bytes 524304 | tf_op jit(solution)/shard_map/reduce_scatter | solution.py:107
  138.0 2.0 %select_convert_fusion = bf16[512,512]{1,0:T(8,128)(2,1)} fusion(bf16[512,512]{1,0:T(8,128)(2,1)} %reduce-scatter.2.cloned.1.call-done, bf16[512,512]{1,0:T(8,128)(2,1)S(1)} %copy-done.3, pred[512]{0:T(512)(128)(4,1)S(1)} %iota_compare_fusion.4), kind=kLoop, calls=%fused_computation.25 | loop fusion | flops 1310720 | bytes 1573376 | tf_op jit(solution)/shard_map/convert_element_type | solution.py:111
  140.0 0.7 copy.36
  (20 shorter events, 0.1 us)
Async XLA Ops:
  7.2 93.8 %copy-start = (bf16[512,2048]{1,0:T(8,128)(2,1)S(1)}, bf16[512,2048]{1,0:T(8,128)(2,1)}, u32[]{:S(2)}) copy-start(bf16[512,2048]{1,0:T(8,128)(2,1)} %param.16) | copy-start | bytes 6291460
  7.2 38.9 %copy-start.2 = (bf16[512,512]{1,0:T(8,128)(2,1)S(1)}, bf16[512,512]{1,0:T(8,128)(2,1)}, u32[]{:S(2)}) copy-start(bf16[512,512]{1,0:T(8,128)(2,1)} %param.12) | copy-start | bytes 1572868
  7.2 18.5 %collective-permute-start = (bf16[512,512]{1,0:T(8,128)(2,1)}, bf16[512,512]{1,0:T(8,128)(2,1)}, u32[]{:S(2)}, u32[]{:S(2)}) collective-permute-start(bf16[512,512]{1,0:T(8,128)(2,1)} %param.12), channel_id=1, source_target_pairs={{0,1},{1,2},{2,3},{3,0},{4,5},{5,6},{6,7},{7,4},{8,9},{9,10},{10,1... | collective-permute-start | bytes 1572872 | tf_op jit(solution)/shard_map/ppermute | solution.py:48
  9.4 34.3 %collective-permute-start.2 = (bf16[512,512]{1,0:T(8,128)(2,1)}, bf16[512,512]{1,0:T(8,128)(2,1)S(1)}, u32[]{:S(2)}, u32[]{:S(2)}) collective-permute-start(bf16[512,512]{1,0:T(8,128)(2,1)} %param.12), channel_id=1, source_target_pairs={{0,3},{1,0},{2,1},{3,2},{4,7},{5,4},{6,5},{7,6},{8,11},{9,8},{10,9... | collective-permute-start | bytes 1572872 | tf_op jit(solution)/shard_map/ppermute | solution.py:50
  10.9 25.7 %all-to-all-start = ((bf16[64,8,256]{2,1,0:T(8,128)(2,1)}), bf16[64,8,256]{2,1,0:T(8,128)(2,1)S(1)}, u32[]{:S(2)}, u32[]{:S(2)}) async-start(bf16[64,8,256]{2,1,0:T(8,128)(2,1)} %param.21), calls=%async_computation | async-start | bytes 524288 | tf_op jit(solution)/shard_map/all_to_all | solution.py:41
  23.5 55.9 %all-gather.2.cloned.1.call-start = ((), (), s32[]{:S(2)}) async-start(), calls=%async_computation.3 | async-start | bytes 1310720 | tf_op jit(solution)/shard_map/all_gather | solution.py:80
  25.7 14.6 %collective-permute-start.1 = (bf16[512,512]{1,0:T(8,128)(2,1)}, bf16[512,512]{1,0:T(8,128)(2,1)}, u32[]{:S(2)}, u32[]{:S(2)}) collective-permute-start(bf16[512,512]{1,0:T(8,128)(2,1)} %collective-permute-done), channel_id=1, source_target_pairs={{0,1},{1,2},{2,3},{3,0},{4,5},{5,6},{6,7},{7,4},{8,9},{9,10},{10,1... | collective-permute-start | bytes 1572872 | tf_op jit(solution)/shard_map/ppermute | solution.py:48
  43.8 3.5 %copy-start.5 = (bf16[2048,256]{1,0:T(8,128)(2,1)S(1)}, bf16[2048,256]{1,0:T(8,128)(2,1)}, u32[]{:S(2)}) copy-start(bf16[2048,256]{1,0:T(8,128)(2,1)} %param.15) | copy-start | bytes 3145732
  43.8 3.5 %copy-start.6 = (f32[2048]{0:T(1024)S(1)}, f32[2048]{0:T(1024)}, u32[]{:S(2)}) copy-start(f32[2048]{0:T(1024)} %param.13) | copy-start | bytes 24580
  46.2 1.9 %copy-start.1 = (bf16[512,4096]{1,0:T(8,128)(2,1)}, bf16[512,4096]{1,0:T(8,128)(2,1)S(1)}, u32[]{:S(2)}) copy-start(bf16[512,4096]{1,0:T(8,128)(2,1)S(1)} %constant_dynamic-update-slice_fusion) | copy-start | bytes 12582916
  52.1 85.9 %reduce-scatter.2.cloned.1.call-start = ((), (), s32[]{:S(2)}) async-start(), calls=%async_computation.4 | async-start | bytes 2621440 | tf_op jit(solution)/shard_map/reduce_scatter | solution.py:107
  83.2 10.7 %copy-start.4 = (bf16[2048,256]{1,0:T(8,128)(2,1)S(1)}, bf16[2048,256]{1,0:T(8,128)(2,1)}, u32[]{:S(2)}) copy-start(bf16[2048,256]{1,0:T(8,128)(2,1)} %bitcast_select_fusion.4) | copy-start | bytes 3145732
  101.0 37.0 %copy-start.3 = (bf16[512,512]{1,0:T(8,128)(2,1)S(1)}, bf16[512,512]{1,0:T(8,128)(2,1)}, u32[]{:S(2)}) copy-start(bf16[512,512]{1,0:T(8,128)(2,1)} %param.12) | copy-start | bytes 1572868
  105.2 24.7 %all-to-all-start.1 = ((bf16[64,8,256]{2,1,0:T(8,128)(2,1)}), bf16[64,8,256]{2,1,0:T(8,128)(2,1)S(1)}, u32[]{:S(2)}, u32[]{:S(2)}) async-start(bf16[64,8,256]{2,1,0:T(8,128)(2,1)} %broadcast_select_fusion), calls=%async_computation.2 | async-start | bytes 524288 | tf_op jit(solution)/shard_map/all_to_all | solution.py:77
Sparse Core Ops, SparseCore 0:
  52.2 27.1 all-gather.1
  103.8 34.1 reduce-scatter.1
